TPU v7x, 128 devices: a whole 4x4x4 slice. The times are simulated.
128 devices in a mesh: dp: 16 (over z, y_hi, core), seq: 8 (over y_lo, x).
Axes of the slice: x: 4, y: 4 (y_hi: 2, y_lo: 2; y = y_hi * 2 + y_lo), z: 4, core: 2. Of those that a mesh axis runs over, the one named last changes fastest.
Arguments:
- tokens: bfloat16 [4096, 4096], P(('dp', 'seq')), may hold values from -6 to 6
- modality: int32 [4096], P(('dp', 'seq')), may hold values from 0 to 1, as said below
- gate_weight: bfloat16 [4096, 14336], P(None, 'dp'), may hold values from -0.09375 to 0.09375
- up_weight: bfloat16 [4096, 14336], P(None, 'dp'), may hold values from -0.09375 to 0.09375
- down_weight: bfloat16 [14336, 4096], P('dp'), may hold values from -0.046875 to 0.046875
- out_grad: bfloat16 [3072, 4096], P(('dp', 'seq')), may hold values from -1.5 to 1.5
Outputs:
- output: bfloat16 [3072, 4096], P(('dp', 'seq'))
- in_grad: bfloat16 [3072, 4096], P(('dp', 'seq'))
- gate_grad: bfloat16 [4096, 14336], P('seq', 'dp')
- up_grad: bfloat16 [4096, 14336], P('seq', 'dp')
- down_grad: bfloat16 [14336, 4096], P('dp', 'seq')
Inputs may be any that keep to these rules, and one draw needn't show every extreme that they name: In each aligned block of 32 tokens (the tokens of one device) exactly 24 tokens have modality 1 (vision); all others have 0 (text).
All inputs are finite; a program needn't handle non-finite values.
Results may differ from a plain program's by a relative error of at most 0.014.
Values may be sent and summed in bfloat16 or wider, within the bound.
A program may use at most 128 MiB of HBM per device.

v0:
```python
import jax
import jax.numpy as jnp
from jax import lax
from jax.sharding import PartitionSpec as P


def silu_parts(gate_proj):
    sigmoid_value = jax.nn.sigmoid(gate_proj)
    return (gate_proj * sigmoid_value, sigmoid_value * (1.0 + gate_proj * (1.0 - sigmoid_value)))


def contract_rows(left_matrix, right_matrix):
    return lax.dot_general(
        left_matrix, right_matrix, (((0,), (0,)), ((), ())), preferred_element_type=jnp.float32
    )


def contract_cols(left_matrix, right_matrix):
    return lax.dot_general(
        left_matrix, right_matrix, (((1,), (1,)), ((), ())), preferred_element_type=jnp.float32
    )


def on_device(tokens, modality, gate_weight, up_weight, down_weight, out_grad):
    vision_count = out_grad.shape[0]
    flags = (modality == 1).astype(jnp.int32)
    ranks = jnp.cumsum(flags) - 1
    slot_ids = jnp.arange(vision_count, dtype=jnp.int32)[:, None]
    selector = ((ranks[None, :] == slot_ids) & (flags[None, :] == 1)).astype(jnp.bfloat16)
    picked = jnp.dot(selector, tokens, preferred_element_type=jnp.float32).astype(jnp.bfloat16)
    token_rows = lax.all_gather(picked, "dp", axis=0, tiled=True)
    gate_proj = jnp.dot(token_rows, gate_weight, preferred_element_type=jnp.float32)
    up_proj = jnp.dot(token_rows, up_weight, preferred_element_type=jnp.float32)
    active, slope = silu_parts(gate_proj)
    hidden = (active * up_proj).astype(jnp.bfloat16)
    output = lax.psum_scatter(
        jnp.dot(hidden, down_weight, preferred_element_type=jnp.float32).astype(jnp.bfloat16),
        "dp",
        scatter_dimension=0,
        tiled=True,
    )
    cotangent_rows = lax.all_gather(out_grad, "dp", axis=0, tiled=True)
    back_hidden = contract_cols(cotangent_rows, down_weight)
    gate_back = (back_hidden * up_proj * slope).astype(jnp.bfloat16)
    up_back = (back_hidden * active).astype(jnp.bfloat16)
    in_grad = lax.psum_scatter(
        (contract_cols(gate_back, gate_weight) + contract_cols(up_back, up_weight)).astype(
            jnp.bfloat16
        ),
        "dp",
        scatter_dimension=0,
        tiled=True,
    )
    gate_part = contract_rows(token_rows, gate_back)
    up_part = contract_rows(token_rows, up_back)
    down_part = contract_rows(hidden, cotangent_rows)
    gate_total, up_total, down_total = (
        lax.psum_scatter(
            gate_part.astype(jnp.bfloat16), "seq", scatter_dimension=0, tiled=True
        ).astype(jnp.float32),
        lax.psum_scatter(
            up_part.astype(jnp.bfloat16), "seq", scatter_dimension=0, tiled=True
        ).astype(jnp.float32),
        lax.psum_scatter(
            down_part.astype(jnp.bfloat16), "seq", scatter_dimension=1, tiled=True
        ).astype(jnp.float32),
    )
    return (
        output,
        in_grad,
        gate_total.astype(jnp.bfloat16),
        up_total.astype(jnp.bfloat16),
        down_total.astype(jnp.bfloat16),
    )


def solution(mesh):
    placed = (
        P(("dp", "seq"), None),
        P(("dp", "seq")),
        P(None, "dp"),
        P(None, "dp"),
        P("dp", None),
        P(("dp", "seq"), None),
    )
    return jax.shard_map(
        on_device,
        mesh=mesh,
        in_specs=placed,
        out_specs=(
            P(("dp", "seq"), None),
            P(("dp", "seq"), None),
            P("seq", "dp"),
            P("seq", "dp"),
            P("dp", "seq"),
        ),
        check_vma=False,
    )
```

profile of v0, /device:TPU:1, one launch (start us, length us, event | category | flops | bytes accessed | tf_op | source)
XLA Modules:
  0.0 548.4 jit_solution(6093787396927904217)
XLA Ops:
  7.2 0.0 all-gather.3.cloned.1.call-start
  7.2 0.7 fusion.5
  7.9 0.1 copy.12
  8.0 0.1 reduce-window.8
  8.1 0.1 add_reduce_fusion
  8.2 0.9 convolution_convert_fusion.4
  9.1 0.0 all-gather.5.cloned.1.call-start
  9.1 0.7 all-gather.5.cloned.1.call-update
  9.8 0.0 reduce-scatter.6.cloned.1.call-start
  9.9 55.7 %all-gather.3.cloned.1.call-done = bf16[384,4096]{1,0:T(8,128)(2,1)} async-done(((bf16[24,4096]{1,0:T(8,128)(2,1)}), bf16[384,4096]{1,0:T(8,128)(2,1)}) %all-gather.3.cloned.1.call-update) | async-done | bytes 3145744 | tf_op jit(solution)/shard_map/all_gather | solution.py:31
  65.6 8.6 %fusion.8 = f32[384,896]{1,0:T(8,128)S(1)} fusion(bf16[384,4096]{1,0:T(8,128)(2,1)} %all-gather.3.cloned.1.call-done, bf16[4096,896]{1,0:T(8,128)(2,1)} %param.9), kind=kOutput, calls=%fused_computation.20 | convolution fusion | flops 2818572288 | bytes 11862016 | tf_op jit(solution)/shard_map/dot_general | solution.py:33
  74.3 5.8 %fusion.7 = f32[384,896]{1,0:T(8,128)S(1)} fusion(bf16[384,4096]{1,0:T(8,128)(2,1)S(1)} %copy-done.2, bf16[4096,896]{1,0:T(8,128)(2,1)} %param.8), kind=kOutput, calls=%fused_computation.19 | convolution fusion | flops 2818572288 | bytes 11862016 | tf_op jit(solution)/shard_map/dot_general | solution.py:32
  80.0 37.6 %all-gather.5.cloned.1.call-done = bf16[384,4096]{1,0:T(8,128)(2,1)} async-done(((bf16[24,4096]{1,0:T(8,128)(2,1)}), bf16[384,4096]{1,0:T(8,128)(2,1)}) %all-gather.5.cloned.1.call-update) | async-done | bytes 3145744 | tf_op jit(solution)/shard_map/all_gather | solution.py:42
  117.7 8.9 %multiply_convert_fusion = (bf16[384,896]{1,0:T(8,128)(2,1)}, bf16[384,896]{1,0:T(8,128)(2,1)}, bf16[384,896]{1,0:T(8,128)(2,1)S(1)}) fusion(f32[384,896]{1,0:T(8,128)S(1)} %fusion.7, f32[384,896]{1,0:T(8,128)S(1)} %fusion.8, bf16[384,4096]{1,0:T(8,128)(2,1)} %all-gather.5.cloned.1.call-done, bf16[896,4096]{1,0:T(8,128)(2,1)} %param.10), kind=kOutput, calls=%fused_computation.6 | convolution fusion | flops 2823733248 | bytes 15302656 | tf_op jit(solution)/shard_map/dot_general | solution.py:19
  126.5 0.8 copy-done.6
  127.4 8.0 %convolution_convert_fusion.3 = bf16[384,4096]{1,0:T(8,128)(2,1)} fusion(bf16[384,896]{1,0:T(8,128)(2,1)S(1)} %get-tuple-element.7, bf16[896,4096]{1,0:T(8,128)(2,1)} %param.10), kind=kOutput, calls=%fused_computation.4 | convolution fusion | flops 2820145152 | bytes 11173888 | tf_op jit(solution)/shard_map/dot_general | solution.py:37
  135.5 0.0 reduce-scatter.8.cloned.1.call-start
  135.5 6.0 %fusion.9 = f32[384,4096]{1,0:T(8,128)S(1)} fusion(bf16[384,896]{1,0:T(8,128)(2,1)} %get-tuple-element.6, bf16[4096,896]{1,0:T(8,128)(2,1)} %param.8), kind=kOutput, calls=%fused_computation.21 | convolution fusion | flops 2818572288 | bytes 14319616 | tf_op jit(solution)/shard_map/dot_general | solution.py:19
  141.6 5.0 add_convert_fusion
  146.6 0.2 reduce-scatter.14.cloned.1.call-start
  146.8 1.8 copy-done.4
  148.6 7.1 %convolution_convert_fusion = bf16[896,4096]{1,0:T(8,128)(2,1)} fusion(bf16[384,896]{1,0:T(8,128)(2,1)} %copy-done.6, bf16[384,4096]{1,0:T(8,128)(2,1)S(1)} %copy-done.4), kind=kOutput, calls=%fused_computation | convolution fusion | flops 2822242304 | bytes 11173888 | tf_op jit(solution)/shard_map/dot_general | solution.py:13
  155.8 0.0 reduce-scatter.12.cloned.1.call-start
  155.8 1.9 copy-done.3
  157.7 7.5 %convolution_convert_fusion.1 = bf16[4096,896]{1,0:T(8,128)(2,1)} fusion(bf16[384,4096]{1,0:T(8,128)(2,1)S(1)} %copy-done.3, bf16[384,896]{1,0:T(8,128)(2,1)} %get-tuple-element.5), kind=kOutput, calls=%fused_computation.1 | convolution fusion | flops 2822242304 | bytes 11173888 | tf_op jit(solution)/shard_map/dot_general | solution.py:13
  165.2 0.0 reduce-scatter.10.cloned.1.call-start
  165.2 7.5 %convolution_convert_fusion.2 = bf16[4096,896]{1,0:T(8,128)(2,1)} fusion(bf16[384,4096]{1,0:T(8,128)(2,1)S(1)} %copy-done.3, bf16[384,896]{1,0:T(8,128)(2,1)} %get-tuple-element.6), kind=kOutput, calls=%fused_computation.2 | convolution fusion | flops 2822242304 | bytes 11173888 | tf_op jit(solution)/shard_map/dot_general | solution.py:13
  172.8 35.4 %reduce-scatter.6.cloned.1.call-done = bf16[24,4096]{1,0:T(8,128)(2,1)} async-done(((bf16[384,4096]{1,0:T(8,128)(2,1)}), bf16[24,4096]{1,0:T(8,128)(2,1)}) %reduce-scatter.6.cloned.1.call-update) | async-done | bytes 196624 | tf_op jit(solution)/shard_map/reduce_scatter | solution.py:36
  208.2 78.8 %reduce-scatter.8.cloned.1.call-done = bf16[24,4096]{1,0:T(8,128)(2,1)} async-done(((bf16[384,4096]{1,0:T(8,128)(2,1)}), bf16[24,4096]{1,0:T(8,128)(2,1)}) %reduce-scatter.8.cloned.1.call-update) | async-done | bytes 196624 | tf_op jit(solution)/shard_map/reduce_scatter | solution.py:46
  286.9 85.6 %reduce-scatter.14.cloned.1.call-done = bf16[896,512]{1,0:T(8,128)(2,1)} async-done(((bf16[896,4096]{1,0:T(8,128)(2,1)}), bf16[896,512]{1,0:T(8,128)(2,1)}) %reduce-scatter.14.cloned.1.call-update) | async-done | bytes 917520 | tf_op jit(solution)/shard_map/reduce_scatter | solution.py:64
  372.5 84.5 %reduce-scatter.12.cloned.1.call-done = bf16[512,896]{1,0:T(8,128)(2,1)} async-done(((bf16[4096,896]{1,0:T(8,128)(2,1)}), bf16[512,896]{1,0:T(8,128)(2,1)}) %reduce-scatter.12.cloned.1.call-update) | async-done | bytes 917520 | tf_op jit(solution)/shard_map/reduce_scatter | solution.py:61
  457.0 84.6 %reduce-scatter.10.cloned.1.call-done = bf16[512,896]{1,0:T(8,128)(2,1)} async-done(((bf16[4096,896]{1,0:T(8,128)(2,1)}), bf16[512,896]{1,0:T(8,128)(2,1)}) %reduce-scatter.10.cloned.1.call-update) | async-done | bytes 917520 | tf_op jit(solution)/shard_map/reduce_scatter | solution.py:58
  (22 shorter events, 0.1 us)
Async XLA Ops:
  7.2 1.0 copy-start
  7.2 58.4 %all-gather.3.cloned.1.call-start = ((), (), s32[]{:S(2)}) async-start(), calls=%async_computation.5 | async-start | bytes 3342336 | tf_op jit(solution)/shard_map/all_gather | solution.py:31
  9.1 108.6 %all-gather.5.cloned.1.call-start = ((), (), s32[]{:S(2)}) async-start(), calls=%async_computation.7 | async-start | bytes 3342336 | tf_op jit(solution)/shard_map/all_gather | solution.py:42
  9.8 198.3 %reduce-scatter.6.cloned.1.call-start = ((), (), s32[]{:S(2)}) async-start(), calls=%async_computation.6 | async-start | bytes 3342336 | tf_op jit(solution)/shard_map/reduce_scatter | solution.py:36
  65.6 8.6 %copy-start.2 = (bf16[384,4096]{1,0:T(8,128)(2,1)S(1)}, bf16[384,4096]{1,0:T(8,128)(2,1)}, u32[]{:S(2)}) copy-start(bf16[384,4096]{1,0:T(8,128)(2,1)} %all-gather.3.cloned.1.call-done) | copy-start | bytes 9437188
  126.5 0.8 copy-start.6
  135.4 6.1 %slice-start = ((s8[7340032]{0:T(1024)(128)(4,1)}), s8[3145728]{0:T(1024)(128)(4,1)S(1)}, s32[]{:S(2)}) async-start(s8[7340032]{0:T(1024)(128)(4,1)} %bitcast.21), calls=%async_computation.12 | async-start | bytes 6291456
  135.5 151.5 %reduce-scatter.8.cloned.1.call-start = ((), (), s32[]{:S(2)}) async-start(), calls=%async_computation.8 | async-start | bytes 3342336 | tf_op jit(solution)/shard_map/reduce_scatter | solution.py:46
  135.5 6.1 %slice-start.1 = ((s8[7340032]{0:T(1024)(128)(4,1)}), s8[4194304]{0:T(1024)(128)(4,1)S(1)}, s32[]{:S(2)}) async-start(s8[7340032]{0:T(1024)(128)(4,1)} %bitcast.21), calls=%async_computation.13 | async-start | bytes 8388608
  135.5 6.1 %copy-start.5 = (bf16[384,896]{1,0:T(8,128)(2,1)S(1)}, bf16[384,896]{1,0:T(8,128)(2,1)}, u32[]{:S(2)}) copy-start(bf16[384,896]{1,0:T(8,128)(2,1)} %get-tuple-element.5) | copy-start | bytes 2064388
  146.6 2.0 copy-start.4
  146.6 225.9 %reduce-scatter.14.cloned.1.call-start = ((), (), s32[]{:S(2)}) async-start(), calls=%async_computation.11 | async-start | bytes 8257536 | tf_op jit(solution)/shard_map/reduce_scatter | solution.py:64
  155.7 1.9 copy-start.3
  155.8 301.2 %reduce-scatter.12.cloned.1.call-start = ((), (), s32[]{:S(2)}) async-start(), calls=%async_computation.10 | async-start | bytes 8257536 | tf_op jit(solution)/shard_map/reduce_scatter | solution.py:61
  165.2 376.4 %reduce-scatter.10.cloned.1.call-start = ((), (), s32[]{:S(2)}) async-start(), calls=%async_computation.9 | async-start | bytes 8257536 | tf_op jit(solution)/shard_map/reduce_scatter | solution.py:58
  172.8 368.8 %copy-start.1 = (bf16[32,4096]{1,0:T(8,128)(2,1)S(1)}, bf16[32,4096]{1,0:T(8,128)(2,1)}, u32[]{:S(2)}) copy-start(bf16[32,4096]{1,0:T(8,128)(2,1)} %param.6) | copy-start | bytes 786436
Sparse Core Ops, SparseCore 0:
  11.0 54.5 all-gather.2
  68.1 49.5 all-gather.4
  135.6 72.5 reduce-scatter.5
  212.7 74.2 reduce-scatter.7
  289.8 82.6 reduce-scatter.13
  375.4 81.5 reduce-scatter.11
  460.0 81.5 reduce-scatter.9
where the time goes:
time: 549 us; the launch traced here: 548 us
  waiting for transfers between devices  463 us (84%)
  matrix products  65.3 us (12%)
  between operations  14.2 us (3%)
    reduce_scatter x1, waiting for transfers between devices, on_device(): lax.psum_scatter(down_part.astype(jnp.bfloat16), 'seq', scatter_dimension...  85.6 us
    reduce_scatter x1, waiting for transfers between devices, on_device(): lax.psum_scatter(gate_part.astype(jnp.bfloat16), 'seq', scatter_dimension...  84.6 us
    reduce_scatter x1, waiting for transfers between devices, on_device(): lax.psum_scatter(up_part.astype(jnp.bfloat16), 'seq', scatter_dimension=0...  84.5 us
    reduce_scatter x1, waiting for transfers between devices, on_device(): lax.psum_scatter((contract_cols(gate_back, gate_weight) + contract_cols(u...  78.8 us
    all_gather x1, waiting for transfers between devices, on_device(): token_rows = lax.all_gather(picked, 'dp', axis=0, tiled=True)  55.7 us
    all_gather x1, waiting for transfers between devices, on_device(): cotangent_rows = lax.all_gather(out_grad, 'dp', axis=0, tiled=True)  37.6 us
    reduce_scatter x1, waiting for transfers between devices, on_device(): lax.psum_scatter(jnp.dot(hidden, down_weight, preferred_element_type=jnp....  35.4 us
    dot_general x3, matrix products, contract_rows(): lax.dot_general(left_matrix, right_matrix, (((0,), (0,)), ((), ())), pref...  22.2 us
  transfers between devices with their start and end apart: 7, of which 7 were waited for; matrix products, arithmetic and copies ran while one was open for 9% of the time, Pallas kernels for 0%

commit v1 on v0

v1 whole, which is shorter than its diff:
```python
import functools

import jax
import jax.numpy as jnp
from jax import lax
from jax.experimental import pallas as pl
from jax.experimental.pallas import tpu as pltpu
from jax.sharding import PartitionSpec as P

MESH = pl.DeviceIdType.MESH
BF16 = jnp.bfloat16
F32 = jnp.float32
ROWS = 48
GROUP = 384
W = 512
FS = 896
D = 4096
PIECES = 4
PIECE = FS // PIECES
SEMS = 176


def dot(a, b):
    return jnp.dot(a, b, preferred_element_type=F32)


def dot_cols(a, b):
    return lax.dot_general(a, b, (((1,), (1,)), ((), ())), preferred_element_type=F32)


def body(sel_ref, place_ref, tok_ref, cot_ref, wg_hbm, wu_hbm, wd_hbm, out_ref, grads_ref,
         wg, wu, wd, flat, cols, ht, swap_out, swap, core_in, z_in, y_in, hid, mid, grad_in,
         weight_sem, send_sem, recv_sem):
    dp, seq = lax.axis_index("dp"), lax.axis_index("seq")
    z, yh, c = dp // 4, (dp // 2) % 2, dp % 2
    yl, x = seq // 4, seq % 4

    def device(dz=0, dyh=0, dc=0, dyl=0, dx=0):
        return {
            "dp": ((z + dz) % 4) * 4 + ((yh + dyh) % 2) * 2 + (c + dc) % 2,
            "seq": ((yl + dyl) % 2) * 4 + (x + dx) % 4,
        }

    sibling = device(dc=1)
    far_y = device(dyh=1)
    near_y = device(dyl=1)
    z_at = {k: device(dz=k) for k in (1, 2, 3)}
    x_at = {k: device(dx=k) for k in (1, 2, 3)}

    loads = [
        pltpu.make_async_copy(s, d, weight_sem.at[i])
        for i, (s, d) in enumerate(((wg_hbm, wg), (wu_hbm, wu), (wd_hbm, wd)))
    ]
    for load in loads:
        load.start()

    barrier = pltpu.get_barrier_semaphore()
    peers = [sibling, far_y, near_y, *z_at.values(), *x_at.values()]
    for peer in peers:
        pl.semaphore_signal(barrier, inc=1, device_id=peer, device_id_type=MESH)

    count = [0]

    def send(src, dst, dev):
        i = count[0]
        count[0] += 1
        copy = pltpu.make_async_remote_copy(
            src_ref=src, dst_ref=dst, send_sem=send_sem.at[i], recv_sem=recv_sem.at[i],
            device_id=dev, device_id_type=MESH,
        )
        copy.start()
        return copy

    other = 1 - c

    def place(half, put):
        for t in range(4):
            at = pl.ds(pl.multiple_of((half * 4 + t) * W, W), W)
            put(1, t, dot(sel_ref[...], tok_ref[:, at]).astype(BF16))
            put(0, t, dot(place_ref[...], cot_ref[:, at]).astype(BF16))

    def put_other(a, t, value):
        swap_out[a, t] = value

    def put_own(a, t, value):
        flat[a, c, t, pl.ds(0, ROWS), :] = value

    place(other, put_other)
    place(c, put_own)

    pl.semaphore_wait(barrier, len(peers))

    def rows(q):
        return pl.ds(q * ROWS, ROWS)

    swaps = [send(swap_out.at[a], swap.at[a], sibling) for a in (1, 0)]

    class Gather:
        def __init__(self, chunk):
            self.chunk = chunk
            self.sent = []

        def put(self, q_src, q_dst, dev, half=None):
            copy = send(self.chunk(q_src, half), self.chunk(q_dst, half), dev)
            self.sent.append(copy)
            return copy

        def stage1(self):
            self.y = self.put(0, 1, far_y)
            self.right = self.put(0, 6, z_at[1])
            self.left = self.put(0, 2, z_at[3])
            self.sib = [self.put(0, 0, sibling)]

        def stage2(self):
            self.y.wait_recv()
            self.right_y = self.put(1, 7, z_at[1])
            self.left_y = self.put(1, 3, z_at[3])
            self.sib.append(self.put(1, 1, sibling))
            self.right.wait_recv()
            self.right2 = self.put(6, 4, z_at[1], 0)
            self.sib.append(self.put(6, 6, sibling))
            self.left.wait_recv()
            self.left2 = self.put(2, 4, z_at[3], 1)
            self.sib.append(self.put(2, 2, sibling))

        def stage3(self):
            self.right_y.wait_recv()
            self.right2_y = self.put(7, 5, z_at[1], 0)
            self.sib.append(self.put(7, 7, sibling))
            self.left_y.wait_recv()
            self.left2_y = self.put(3, 5, z_at[3], 1)
            self.sib.append(self.put(3, 3, sibling))

        def stage4(self):
            self.right2.wait_recv()
            self.left2.wait_recv()
            self.sib.append(self.put(4, 4, sibling))
            self.right2_y.wait_recv()
            self.left2_y.wait_recv()
            self.sib.append(self.put(5, 5, sibling))

        def finish(self):
            for copy in self.sib:
                copy.wait_recv()

        def sources_free(self):
            for copy in self.sent:
                copy.wait_send()

    def row_chunk(a):
        def chunk(q, half):
            if half is None:
                return flat.at[a, c, :, rows(q), :]
            return flat.at[a, c, :, rows(q), pl.ds(half * 256, 256)]
        return chunk

    def col_chunk(a):
        def chunk(q, half):
            lanes = pl.ds(0, W) if half is None else pl.ds(half * 256, 256)
            return cols.at[a, c, pl.ds(1, 3), rows(q), lanes]
        return chunk

    tok_rows, cot_rows = Gather(row_chunk(1)), Gather(row_chunk(0))
    tok_cols, cot_cols = Gather(col_chunk(1)), Gather(col_chunk(0))
    spread = {1: [], 0: []}

    def own_rows(a, copy):
        copy.wait_recv()
        for t in range(4):
            flat[a, c, t, rows(0), :] = flat[a, c, t, rows(0), :] + swap[a, t]

    def spread_cols(a):
        for e in (1, 3, 2):
            spread[a].append(
                send(flat.at[a, c, (x + e) % 4, rows(0), :], cols.at[a, c, 4 - e, rows(0), :], x_at[e])
            )

    own_rows(1, swaps[0])
    own_rows(0, swaps[1])
    tok_rows.stage1()
    spread_cols(1)
    spread_cols(0)
    tok_rows.stage2()
    cot_rows.stage1()
    tok_rows.stage3()
    tok_rows.stage4()
    tok_rows.finish()

    def project(weight, dst):
        def step(k, _):
            part = dot(flat[1, k // 4, k % 4], weight[pl.ds(pl.multiple_of(k * W, W), W), :])
            mid[dst] = mid[dst] + part
            return 0
        mid[dst] = jnp.zeros((GROUP, FS), F32)
        lax.fori_loop(0, 8, step, 0)

    loads[0].wait()
    project(wg, 0)
    cot_rows.stage2()
    loads[1].wait()
    project(wu, 1)

    def tiles(fn):
        for j in range(FS // 128):
            fn(pl.ds(j * 128, 128))

    def forward(at):
        gate, up = mid[0, :, at], mid[1, :, at]
        sig = jax.nn.sigmoid(gate)
        active = gate * sig
        value = active * up
        hid[0, :, at] = value.astype(BF16)
        ht[0, at, pl.ds(0, GROUP)] = value.T.astype(BF16)
        mid[0, :, at] = active
        mid[1, :, at] = up * (sig * (1.0 + gate * (1.0 - sig)))

    tiles(forward)

    def piece(m, p, d, half=None):
        if half is None:
            return ht.at[m, pl.ds(p * PIECE, PIECE), pl.ds(d * GROUP, GROUP)]
        return ht.at[m, pl.ds(p * PIECE + half * (PIECE // 2), PIECE // 2), pl.ds(d * GROUP, GROUP)]

    ring = {}
    ring2 = {}

    def ring_start(m):
        for p in range(PIECES):
            ring[m, p] = (send(piece(m, p, 0), piece(m, p, 3), x_at[1]), send(piece(m, p, 0), piece(m, p, 1), x_at[3]))

    def ring_pass(m, p):
        right, left = ring[m, p]
        right.wait_recv()
        a = send(piece(m, p, 3, 0), piece(m, p, 2, 0), x_at[1])
        left.wait_recv()
        b = send(piece(m, p, 1, 1), piece(m, p, 2, 1), x_at[3])
        ring2[m, p] = (a, b)

    ring_start(0)
    cot_rows.stage3()
    cot_rows.stage4()
    for copy in spread[0]:
        copy.wait_recv()
    cot_cols.stage1()
    cot_rows.finish()

    loads[2].wait()

    def back_step(k, _):
        part = dot_cols(flat[0, k // 4, k % 4], wd[:, pl.ds(pl.multiple_of(k * W, W), W)])
        hidden_back[...] = hidden_back[...] + part
        return 0

    hidden_back = mid.at[2]
    hidden_back[...] = jnp.zeros((GROUP, FS), F32)
    lax.fori_loop(0, 8, back_step, 0)
    cot_cols.stage2()

    def backward(at):
        back = mid[2, :, at]
        gate_back = back * mid[1, :, at]
        up_back = back * mid[0, :, at]
        hid[1, :, at] = gate_back.astype(BF16)
        hid[2, :, at] = up_back.astype(BF16)
        ht[1, at, pl.ds(0, GROUP)] = gate_back.T.astype(BF16)
        ht[2, at, pl.ds(0, GROUP)] = up_back.T.astype(BF16)

    tiles(backward)
    ring_start(1)
    ring_start(2)
    ring_pass(0, 0)
    cot_cols.stage3()
    ring_pass(0, 1)
    for copy in spread[1]:
        copy.wait_recv()
    tok_cols.stage1()
    cot_cols.stage4()

    for a in range(2):
        for h in range(2):
            cols[a, h, 0] = flat[a, h, x]
    for gather in (tok_rows, cot_rows):
        gather.sources_free()
    for a in range(2):
        for copy in spread[a]:
            copy.wait_send()

    def out_tile(h, t):
        k = h * 4 + t
        at = pl.ds(pl.multiple_of(k * W, W), W)
        flat[0, h, t] = dot(hid[0], wd[:, at]).astype(BF16)
        flat[1, h, t] = (dot_cols(hid[1], wg[at, :]) + dot_cols(hid[2], wu[at, :])).astype(BF16)

    def out_half(h):
        def step(t, _):
            out_tile(h, t)
            return 0
        lax.fori_loop(0, 4, step, 0)

    out_half(other)
    to_core = send(flat.at[:, other], core_in, sibling)
    ring_pass(0, 2)
    tok_cols.stage2()
    out_half(c)
    ring_pass(0, 3)
    tok_cols.stage3()
    cot_cols.finish()

    partner = {}

    def weight_grad(m, p):
        for copy in ring2[m, p]:
            copy.wait_recv()
        a = 0 if m == 0 else 1
        at = pl.ds(p * PIECE, PIECE)
        lhs = ht[m, at, :]
        theirs = wd.at[at, pl.ds(m * W, W)]
        theirs[...] = dot(lhs, cols[a, 1 - yl].reshape(4 * GROUP, W)).astype(BF16)
        partner[m, p] = send(theirs, grad_in.at[m, at, :], near_y)
        grads_ref[m, at, :] = dot(lhs, cols[a, yl].reshape(4 * GROUP, W)).astype(BF16)

    def weight_done(m, p):
        partner[m, p].wait_recv()
        at = pl.ds(p * PIECE, PIECE)
        grads_ref[m, at, :] = (grads_ref[m, at, :].astype(F32) + grad_in[m, at, :].astype(F32)).astype(BF16)

    weight_grad(0, 0)
    tok_cols.stage4()
    to_core.wait_recv()
    for a in range(2):
        for t in range(4):
            flat[a, c, t] = (flat[a, c, t].astype(F32) + core_in[a, t].astype(F32)).astype(BF16)
    to_z = {
        e: send(flat.at[:, c, :, pl.ds(e * 2 * ROWS, 2 * ROWS), :], z_in.at[e - 1], z_at[e]) for e in (1, 3, 2)
    }
    weight_grad(0, 1)
    weight_grad(0, 2)
    ring_pass(1, 0)
    weight_grad(0, 3)
    tok_cols.finish()

    order = [(m, p) for m in range(3) for p in range(PIECES)]
    finals = {}

    def z_done():
        for e in (1, 2, 3):
            to_z[e].wait_recv()
        for a in range(2):
            for t in range(4):
                total = flat[a, c, t, pl.ds(0, 2 * ROWS), :].astype(F32)
                for e in range(3):
                    total = total + z_in[e, a, t].astype(F32)
                flat[a, c, t, pl.ds(0, 2 * ROWS), :] = total.astype(BF16)
        finals["y"] = send(flat.at[:, c, :, rows(1), :], y_in, far_y)

    def y_done():
        finals["y"].wait_recv()
        for a in range(2):
            for t in range(4):
                out_ref[a, c, t] = (
                    flat[a, c, t, rows(0), :].astype(F32) + y_in[a, t].astype(F32)
                ).astype(BF16)
        finals["core"] = send(out_ref.at[:, c], out_ref.at[:, c], sibling)

    for i in range(4, 12):
        if i + 1 < 12:
            ring_pass(*order[i + 1])
        weight_grad(*order[i])
        weight_done(*order[i - 4])
        if i == 8:
            z_done()
        if i == 10:
            y_done()
    for i in range(8, 12):
        weight_done(*order[i])

    finals["core"].wait()
    for copy in swaps:
        copy.wait_send()
    finals["y"].wait_send()
    to_core.wait_send()
    for copy in to_z.values():
        copy.wait_send()
    for key in order:
        partner[key].wait_send()
        for copy in (*ring[key], *ring2[key]):
            copy.wait_send()
    for gather in (tok_cols, cot_cols):
        gather.sources_free()


def on_device(tokens, modality, gate_weight, up_weight, down_weight, out_grad):
    count = out_grad.shape[0]
    c = lax.axis_index("dp") % 2
    flags = modality == 1
    here = jnp.arange(tokens.shape[0], dtype=jnp.int32)
    ranks = jnp.sum((here[None, :] < here[:, None]) & flags[None, :], axis=1).astype(jnp.int32)
    slots = jnp.arange(2 * count, dtype=jnp.int32)[:, None] - c * count
    sel = ((ranks[None, :] == slots) & flags[None, :]).astype(BF16)
    place = (jnp.arange(count, dtype=jnp.int32)[None, :] == slots).astype(BF16)
    vmem, hbm = pl.BlockSpec(memory_space=pltpu.VMEM), pl.BlockSpec(memory_space=pltpu.HBM)
    out, grads = pl.pallas_call(
        body,
        out_shape=(
            jax.ShapeDtypeStruct((2, 2, 4, ROWS, W), BF16),
            jax.ShapeDtypeStruct((3, FS, W), BF16),
        ),
        in_specs=[vmem] * 4 + [hbm] * 3,
        out_specs=(vmem, vmem),
        scratch_shapes=[
            pltpu.VMEM((D, FS), BF16),
            pltpu.VMEM((D, FS), BF16),
            pltpu.VMEM((FS, D), BF16),
            pltpu.VMEM((2, 2, 4, GROUP, W), BF16),
            pltpu.VMEM((2, 2, 4, GROUP, W), BF16),
            pltpu.VMEM((3, FS, 4 * GROUP), BF16),
            pltpu.VMEM((2, 4, ROWS, W), BF16),
            pltpu.VMEM((2, 4, ROWS, W), BF16),
            pltpu.VMEM((2, 4, GROUP, W), BF16),
            pltpu.VMEM((3, 2, 4, 2 * ROWS, W), BF16),
            pltpu.VMEM((2, 4, ROWS, W), BF16),
            pltpu.VMEM((3, GROUP, FS), BF16),
            pltpu.VMEM((3, GROUP, FS), F32),
            pltpu.VMEM((3, FS, W), BF16),
            pltpu.SemaphoreType.DMA((3,)),
            pltpu.SemaphoreType.DMA((SEMS,)),
            pltpu.SemaphoreType.DMA((SEMS,)),
        ],
        compiler_params=pltpu.CompilerParams(
            collective_id=0, has_side_effects=True, vmem_limit_bytes=62 * 1024 * 1024
        ),
        name="ffn",
    )(sel, place, tokens, out_grad, gate_weight, up_weight, down_weight)
    rows = lax.dynamic_slice_in_dim(out, c * count, count, axis=3)
    rows = rows.transpose(0, 3, 1, 2, 4).reshape(2, count, D)
    return rows[0], rows[1], grads[1].T, grads[2].T, grads[0]


def solution(mesh):
    return jax.shard_map(
        on_device,
        mesh=mesh,
        in_specs=(
            P(("dp", "seq"), None),
            P(("dp", "seq")),
            P(None, "dp"),
            P(None, "dp"),
            P("dp", None),
            P(("dp", "seq"), None),
        ),
        out_specs=(
            P(("dp", "seq"), None),
            P(("dp", "seq"), None),
            P("seq", "dp"),
            P("seq", "dp"),
            P("dp", "seq"),
        ),
        check_vma=False,
    )
```

time: 549 us -> 178 us (0.32)
  waiting for transfers between devices: 463 us -> 0 us
  Pallas kernels: 0 us -> 166 us
  matrix products: 65.3 us -> 0 us
  between operations: 14.2 us -> 0.69 us
    reduce_scatter x5 -> x0, waiting for transfers between devices: 369 us -> none  [the longest x1 85.6 us: on_device(): lax.psum_scatter(down_part.astype(jnp.bfloat16), 'seq', scatter_dimension...]
    pallas_call x0 -> x1, Pallas kernels: none -> 166 us  [on_device(): pl.pallas_call(body, out_shape=(jax.ShapeDtypeStruct((2, 2, 4, ROWS, W),...]
    all_gather x2 -> x0, waiting for transfers between devices: 93.4 us -> none  [the longest x1 55.7 us: on_device(): token_rows = lax.all_gather(picked, 'dp', axis=0, tiled=True)]
    dot_general x10 -> x0, matrix products: 65.3 us -> none  [the longest x3 22.2 us: contract_rows(): lax.dot_general(left_matrix, right_matrix, (((0,), (0,)), ((), ())), pref...]
  transfers between devices with their start and end apart: 7 -> 0, of which waited for: 7 -> 0; matrix products, arithmetic and copies ran while one was open for 9% -> 0% of each run, Pallas kernels for 0% -> 0%
where the time goes in v1:
time: 178 us
  Pallas kernels  166 us (93%)
  local copies, waits for them, and re-layouts  8.24 us (5%)
  other arithmetic  2.14 us (1%)
    pallas_call x1, Pallas kernels, on_device(): pl.pallas_call(body, out_shape=(jax.ShapeDtypeStruct((2, 2, 4, ROWS, W),...  166 us
    squeeze x3, local copies, waits for them, and re-layouts, on_device(): return (rows[0], rows[1], grads[1].T, grads[2].T, grads[0])  4.44 us

profile of v1, /device:TPU:1, one launch (start us, length us, event | category | flops | bytes accessed | tf_op | source)
XLA Modules:
  0.0 177.5 jit_solution(1565653228244108738)
XLA Ops:
  0.7 0.7 broadcast_compare_fusion
  1.3 0.1 convert_reduce_fusion
  1.4 0.7 and_convert_fusion.sel_ref
  2.1 0.7 fusion.place_ref
  2.8 166.4 %ffn.1 = (bf16[2,2,4,48,512]{4,3,2,1,0:T(8,128)(2,1)}, bf16[3,896,512]{2,1,0:T(8,128)(2,1)}) custom-call(bf16[48,32]{1,0:T(8,128)(2,1)} %and_convert_fusion.sel_ref, bf16[48,24]{1,0:T(8,128)(2,1)} %fusion.place_ref, bf16[32,4096]{1,0:T(8,128)(2,1)} %tok_ref.1, bf16[24,4096]{1,0:T(8,128)(2,1)} %cot_ref.1, bf16[4096,896]{1,0:T(8,128)(2,1)} %wg_hbm.1, ...), custom_call_target="tpu_custom_call" | custom-call | tf_op jit(solution)/shard_map/ffn/pallas_call | solution.py:402
  169.2 1.0 dynamic-slice_bitcast_fusion
  170.3 0.1 copy.18
  170.4 0.8 squeeze.16
  171.2 0.1 copy.17
  171.3 0.8 squeeze.15
  172.1 2.8 %slice_bitcast_fusion = (bf16[896,512]{1,0:T(8,128)(2,1)}, bf16[512,896]{0,1:T(8,128)(2,1)S(1)}, bf16[512,896]{0,1:T(8,128)(2,1)S(1)}) fusion(bf16[3,896,512]{2,1,0:T(8,128)(2,1)} %get-tuple-element.8), kind=kLoop, calls=%fused_computation | loop fusion | bytes 5505024 | tf_op jit(solution)/shard_map/squeeze | solution.py:436
  175.0 1.3 copy.20
  176.2 1.3 copy.19
  (2 shorter events, 0.0 us)

commit v2 on v1

v2 whole, which is shorter than its diff:
```python
import functools

import jax
import jax.numpy as jnp
from jax import lax
from jax.experimental import pallas as pl
from jax.experimental.pallas import tpu as pltpu
from jax.sharding import PartitionSpec as P

MESH = pl.DeviceIdType.MESH
BF16 = jnp.bfloat16
F32 = jnp.float32
ROWS = 48
GROUP = 384
W = 512
FS = 896
D = 4096
PIECES = ((0, 256), (256, 256), (512, 256), (768, 128))
SEMS = 176


def dot(a, b):
    return jnp.dot(a, b, preferred_element_type=F32)


def dot_cols(a, b):
    return lax.dot_general(a, b, (((1,), (1,)), ((), ())), preferred_element_type=F32)


def body(flag_ref, tok_ref, cot_ref, wg_hbm, wu_hbm, wd_hbm,
         out_ref, in_ref, gate_ref, up_ref, down_ref,
         wg, wu, wd, flat, cols, ht, swap, core_in, z_in, y_in, final, final_out, hid, mid, grad_in,
         weight_sem, send_sem, recv_sem):
    dp, seq = lax.axis_index("dp"), lax.axis_index("seq")
    z, yh, c = dp // 4, (dp // 2) % 2, dp % 2
    yl, x = seq // 4, seq % 4
    other = 1 - c

    def device(dz=0, dyh=0, dc=0, dyl=0, dx=0):
        return {
            "dp": ((z + dz) % 4) * 4 + ((yh + dyh) % 2) * 2 + (c + dc) % 2,
            "seq": ((yl + dyl) % 2) * 4 + (x + dx) % 4,
        }

    sibling = device(dc=1)
    far_y = device(dyh=1)
    near_y = device(dyl=1)
    z_at = {k: device(dz=k) for k in (1, 2, 3)}
    x_at = {k: device(dx=k) for k in (1, 2, 3)}

    loads = [
        pltpu.make_async_copy(s, d, weight_sem.at[i])
        for i, (s, d) in enumerate(((wg_hbm, wg), (wu_hbm, wu), (wd_hbm, wd)))
    ]
    for load in loads:
        load.start()

    barrier = pltpu.get_barrier_semaphore()
    peers = [sibling, far_y, near_y, *z_at.values(), *x_at.values()]
    for peer in peers:
        pl.semaphore_signal(barrier, inc=1, device_id=peer, device_id_type=MESH)

    count = [0]

    def send(src, dst, dev):
        i = count[0]
        count[0] += 1
        copy = pltpu.make_async_remote_copy(
            src_ref=src, dst_ref=dst, send_sem=send_sem.at[i], recv_sem=recv_sem.at[i],
            device_id=dev, device_id_type=MESH,
        )
        copy.start()
        return copy

    def rows(q):
        return pl.ds(q * ROWS, ROWS)

    tokens, cots = tok_ref.shape[0], cot_ref.shape[0]

    def grid(shape, dim):
        return lax.broadcasted_iota(jnp.int32, shape, dim)

    flags = (flag_ref[...] == 1).astype(F32)
    before = (grid((tokens, tokens), 0) < grid((tokens, tokens), 1)).astype(F32)
    ranks = dot(jnp.broadcast_to(flags, (8, tokens)), before)[0:1]
    slots = (grid((2 * cots, tokens), 0) - c * cots).astype(F32)
    sel = jnp.where(slots == ranks, flags, 0.0).astype(BF16)
    place_cots = (grid((2 * cots, cots), 0) - c * cots == grid((2 * cots, cots), 1)).astype(BF16)

    def place(a, half, put):
        for t in range(4):
            at = pl.ds(pl.multiple_of((half * 4 + t) * W, W), W)
            put(a, t, (dot(sel, tok_ref[:, at]) if a else dot(place_cots, cot_ref[:, at])).astype(BF16))

    def put_other(a, t, value):
        core_in[a, t, rows(0), :] = value

    def put_own(a, t, value):
        flat[a, c, t, rows(0), :] = value

    place(1, other, put_other)
    place(1, c, put_own)

    pl.semaphore_wait(barrier, len(peers))
    swaps = {1: send(core_in.at[1, :, rows(0), :], swap.at[1], sibling)}
    place(0, other, put_other)
    swaps[0] = send(core_in.at[0, :, rows(0), :], swap.at[0], sibling)
    place(0, c, put_own)
    class Gather:
        def __init__(self, chunk):
            self.chunk = chunk
            self.sent = []

        def put(self, q_src, q_dst, dev, half=None):
            copy = send(self.chunk(q_src, half), self.chunk(q_dst, half), dev)
            self.sent.append(copy)
            return copy

        def first_y(self):
            self.y = self.put(0, 1, far_y)
            self.sib = [self.put(0, 0, sibling)]

        def first_z(self):
            self.right = self.put(0, 6, z_at[1])
            self.left = self.put(0, 2, z_at[3])

        def stage2(self):
            self.right.wait_recv()
            self.right2 = self.put(6, 4, z_at[1], 0)
            self.over = [self.put(6, 7, far_y)]
            self.left.wait_recv()
            self.left2 = self.put(2, 4, z_at[3], 1)
            self.over.append(self.put(2, 3, far_y))
            self.sib += [self.put(6, 6, sibling), self.put(2, 2, sibling)]
            self.y.wait_recv()
            self.sib.append(self.put(1, 1, sibling))

        def stage3(self):
            self.right2.wait_recv()
            self.left2.wait_recv()
            self.over.append(self.put(4, 5, far_y))
            self.sib.append(self.put(4, 4, sibling))
            for copy, q in zip(self.over, (7, 3)):
                copy.wait_recv()
                self.sib.append(self.put(q, q, sibling))

        def stage4(self):
            self.over[2].wait_recv()
            self.sib.append(self.put(5, 5, sibling))

        def finish(self):
            for copy in self.sib:
                copy.wait_recv()

        def sources_free(self):
            for copy in self.sent:
                copy.wait_send()

    class GatherZ(Gather):
        def stage2(self):
            self.y.wait_recv()
            self.right_y = self.put(1, 7, z_at[1])
            self.left_y = self.put(1, 3, z_at[3])
            self.sib.append(self.put(1, 1, sibling))
            self.right.wait_recv()
            self.right2 = self.put(6, 4, z_at[1], 0)
            self.sib.append(self.put(6, 6, sibling))
            self.left.wait_recv()
            self.left2 = self.put(2, 4, z_at[3], 1)
            self.sib.append(self.put(2, 2, sibling))

        def stage3(self):
            self.right_y.wait_recv()
            self.right2_y = self.put(7, 5, z_at[1], 0)
            self.sib.append(self.put(7, 7, sibling))
            self.left_y.wait_recv()
            self.left2_y = self.put(3, 5, z_at[3], 1)
            self.sib.append(self.put(3, 3, sibling))

        def stage4(self):
            self.right2.wait_recv()
            self.left2.wait_recv()
            self.sib.append(self.put(4, 4, sibling))
            self.right2_y.wait_recv()
            self.left2_y.wait_recv()
            self.sib.append(self.put(5, 5, sibling))

    def row_chunk(a):
        def chunk(q, half):
            if half is None:
                return flat.at[a, c, :, rows(q), :]
            return flat.at[a, c, :, rows(q), pl.ds(half * 256, 256)]
        return chunk

    def col_chunk(a):
        def chunk(q, half):
            lanes = pl.ds(0, W) if half is None else pl.ds(half * 256, 256)
            return cols.at[a, c, pl.ds(1, 3), rows(q), lanes]
        return chunk

    tok_rows, cot_rows = GatherZ(row_chunk(1)), GatherZ(row_chunk(0))
    tok_cols, cot_cols = GatherZ(col_chunk(1)), GatherZ(col_chunk(0))
    spread = {1: [], 0: []}

    def own_rows(a):
        swaps[a].wait()
        for t in range(4):
            flat[a, c, t, rows(0), :] = flat[a, c, t, rows(0), :] + swap[a, t]

    def spread_cols(a):
        for e in (1, 3, 2):
            spread[a].append(
                send(flat.at[a, c, (x + e) % 4, rows(0), :], cols.at[a, c, 4 - e, rows(0), :], x_at[e])
            )

    def own_cols(a):
        for h in range(2):
            cols[a, h, 0] = flat[a, h, x]

    def rows_free(a, gather):
        gather.sources_free()
        for copy in spread[a]:
            copy.wait_send()

    def start_cols(a, gather):
        for copy in spread[a]:
            copy.wait_recv()
        gather.first_y()

    def project(weight, dst):
        def step(k, _):
            mid[dst] = mid[dst] + dot(flat[1, k // 4, k % 4], weight[pl.ds(pl.multiple_of(k * W, W), W), :])
            return 0
        mid[dst] = dot(flat[1, 0, 0], weight[pl.ds(0, W), :])
        lax.fori_loop(1, 8, step, 0)

    def project_back():
        def step(k, _):
            mid[2] = mid[2] + dot_cols(flat[0, k // 4, k % 4], wd[:, pl.ds(pl.multiple_of(k * W, W), W)])
            return 0
        mid[2] = dot_cols(flat[0, 0, 0], wd[:, pl.ds(0, W)])
        lax.fori_loop(1, 8, step, 0)

    def tiles(fn):
        for j in range(FS // 128):
            fn(pl.ds(j * 128, 128))

    def forward(at):
        gate, up = mid[0, :, at], mid[1, :, at]
        sig = jax.nn.sigmoid(gate)
        active = gate * sig
        value = active * up
        hid[0, :, at] = value.astype(BF16)
        ht[0, at, pl.ds(0, GROUP)] = value.T.astype(BF16)
        mid[0, :, at] = active
        mid[1, :, at] = up * (sig * (1.0 + gate * (1.0 - sig)))

    def backward(at):
        back = mid[2, :, at]
        gate_back = back * mid[1, :, at]
        up_back = back * mid[0, :, at]
        hid[1, :, at] = gate_back.astype(BF16)
        hid[2, :, at] = up_back.astype(BF16)
        ht[1, at, pl.ds(0, GROUP)] = gate_back.T.astype(BF16)
        ht[2, at, pl.ds(0, GROUP)] = up_back.T.astype(BF16)

    order = [(m, p) for m in range(3) for p in range(len(PIECES))]

    def piece(i, d, half=None):
        m, (start, size) = order[i][0], PIECES[order[i][1]]
        if half is not None:
            size //= 2
            start += half * size
        return ht.at[m, pl.ds(start, size), pl.ds(d * GROUP, GROUP)]

    ring, ring2, partner = {}, {}, {}

    def ring_start(i):
        ring[i] = (send(piece(i, 0), piece(i, 3), x_at[1]), send(piece(i, 0), piece(i, 1), x_at[3]))

    def ring_pass(i):
        right, left = ring[i]
        right.wait_recv()
        a = send(piece(i, 3, 0), piece(i, 2, 0), x_at[1])
        left.wait_recv()
        b = send(piece(i, 1, 1), piece(i, 2, 1), x_at[3])
        ring2[i] = (a, b)

    def parts(i):
        m, (start, size) = order[i][0], PIECES[order[i][1]]
        at = pl.ds(start, size)
        own = down_ref.at[at, :] if m == 0 else wd.at[at, pl.ds((3 + m) * W, W)]
        theirs = gate_ref.at[at, pl.ds(0, W)] if i == 0 else wd.at[at, pl.ds(m * W, W)]
        return m, at, theirs, own

    def weight_grad(i):
        for copy in ring2[i]:
            copy.wait_recv()
        m, at, theirs, own = parts(i)
        a = 0 if m == 0 else 1
        lhs = ht[m, at, :]
        theirs[...] = dot(lhs, cols[a, 1 - yl].reshape(4 * GROUP, W)).astype(BF16)
        partner[i] = send(theirs, grad_in.at[m, at, :], near_y)
        own[...] = dot(lhs, cols[a, yl].reshape(4 * GROUP, W)).astype(BF16)

    def weight_done(i):
        partner[i].wait()
        m, at, theirs, own = parts(i)
        total = own[...].astype(F32) + grad_in[m, at, :].astype(F32)
        if m == 0:
            down_ref[at, :] = total.astype(BF16)
        elif m == 1:
            gate_ref[:, at] = total.T.astype(BF16)
        else:
            up_ref[:, at] = total.T.astype(BF16)

    def out_half(h):
        def step(t, _):
            at = pl.ds(pl.multiple_of((h * 4 + t) * W, W), W)
            flat[1, h, t] = dot(hid[0], wd[:, at]).astype(BF16)
            return 0
        lax.fori_loop(0, 4, step, 0)

    def in_half(h):
        def step(t, _):
            at = pl.ds(pl.multiple_of((h * 4 + t) * W, W), W)
            flat[0, h, t] = (dot_cols(hid[1], wg[at, :]) + dot_cols(hid[2], wu[at, :])).astype(BF16)
            return 0
        lax.fori_loop(0, 4, step, 0)

    to_core, to_z, to_y, to_own = {}, {}, {}, {}

    def core_start(a):
        to_core[a] = send(flat.at[a, other], core_in.at[a], sibling)

    def core_done(a):
        to_core[a].wait_recv()
        for t in range(4):
            flat[a, c, t] = (flat[a, c, t].astype(F32) + core_in[a, t].astype(F32)).astype(BF16)
        to_z[a] = {
            e: send(flat.at[a, c, :, pl.ds(e * 2 * ROWS, 2 * ROWS), :], z_in.at[e - 1, a], z_at[e]) for e in (1, 3, 2)
        }

    def z_done(a):
        for e in (1, 2, 3):
            to_z[a][e].wait_recv()
        for t in range(4):
            total = flat[a, c, t, pl.ds(0, 2 * ROWS), :].astype(F32)
            for e in range(3):
                total = total + z_in[e, a, t].astype(F32)
            flat[a, c, t, pl.ds(0, 2 * ROWS), :] = total.astype(BF16)
        to_y[a] = send(flat.at[a, c, :, rows(1), :], y_in.at[a], far_y)

    def y_done(a):
        to_y[a].wait_recv()
        ref = out_ref if a else in_ref
        for t in range(4):
            final[...] = flat[a, c, t, rows(0), :].astype(F32) + y_in[a, t].astype(F32)
            at = pl.ds(pl.multiple_of((c * 4 + t) * W, W), W)
            ref[:, at] = final[pl.ds(pl.multiple_of(c * cots, 8), cots), :].astype(BF16)
            final_out[a, :, pl.ds(t * W, W)] = final[pl.ds(pl.multiple_of(other * cots, 8), cots), :].astype(BF16)
        half = pl.ds(pl.multiple_of(c * 4 * W, W), 4 * W)
        to_own[a] = send(final_out.at[a], ref.at[:, half], sibling)

    own_rows(1)
    tok_rows.first_y()
    tok_rows.first_z()
    spread_cols(1)
    own_rows(0)
    spread_cols(0)
    cot_rows.first_y()
    tok_rows.stage2()
    start_cols(0, cot_cols)
    tok_rows.stage3()
    cot_cols.first_z()
    tok_rows.stage4()
    cot_rows.first_z()
    tok_rows.finish()
    own_cols(1)
    loads[0].wait()
    project(wg, 0)
    cot_cols.stage2()
    loads[1].wait()
    project(wu, 1)
    tiles(forward)
    ring_start(0)
    ring_start(1)
    cot_rows.stage2()
    cot_cols.stage3()
    rows_free(1, tok_rows)
    loads[2].wait()
    out_half(other)
    core_start(1)
    ring_pass(0)
    ring_start(2)
    cot_rows.stage3()
    cot_cols.stage4()
    start_cols(1, tok_cols)
    tok_cols.first_z()
    ring_pass(1)
    ring_start(3)
    out_half(c)
    cot_rows.stage4()
    cot_rows.finish()
    own_cols(0)
    cot_cols.finish()
    ring_pass(2)
    tok_cols.stage2()
    weight_grad(0)
    project_back()
    tiles(backward)
    ring_start(4)
    ring_start(5)
    ring_pass(3)
    weight_grad(1)
    tok_cols.stage3()
    rows_free(0, cot_rows)
    in_half(other)
    core_start(0)
    weight_grad(2)
    ring_pass(4)
    ring_start(6)
    tok_cols.stage4()
    core_done(1)
    weight_grad(3)
    ring_pass(5)
    ring_start(7)
    tok_cols.finish()
    weight_grad(4)
    in_half(c)
    ring_pass(6)
    ring_start(8)
    weight_grad(5)
    core_done(0)
    ring_pass(7)
    ring_start(9)
    for i in range(6, 12):
        weight_grad(i)
        if i + 2 < 12:
            ring_pass(i + 2)
        if i + 4 < 12:
            ring_start(i + 4)
        weight_done(i - 6)
        if i == 6:
            z_done(1)
        if i == 8:
            y_done(1)
        if i == 9:
            z_done(0)
        if i == 11:
            y_done(0)
    for i in (6, 7):
        weight_done(i)
    for i in range(8, 12):
        weight_done(i)
    for a in (1, 0):
        to_own[a].wait()
        to_y[a].wait_send()
        to_core[a].wait_send()
        for copy in to_z[a].values():
            copy.wait_send()
    for i in range(12):
        for copy in (*ring[i], *ring2[i]):
            copy.wait_send()
    for gather in (tok_cols, cot_cols):
        gather.sources_free()


def store(*refs):
    held, sems = refs[10:15], refs[15]
    loads = [pltpu.make_async_copy(refs[i], held[i], sems.at[i]) for i in range(5)]
    stores = [pltpu.make_async_copy(held[i], refs[5 + i], sems.at[5 + i]) for i in range(5)]
    for copy in loads:
        copy.start()
    for load, copy in zip(loads, stores):
        load.wait()
        copy.start()
    for copy in stores:
        copy.wait()


def on_device(tokens, modality, gate_weight, up_weight, down_weight, out_grad):
    vmem, hbm = pl.BlockSpec(memory_space=pltpu.VMEM), pl.BlockSpec(memory_space=pltpu.HBM)
    count = out_grad.shape[0]
    out, in_grad, gate_grad, up_grad, down_grad = pl.pallas_call(
        body,
        out_shape=(
            jax.ShapeDtypeStruct((count, D), BF16),
            jax.ShapeDtypeStruct((count, D), BF16),
            jax.ShapeDtypeStruct((W, FS), BF16),
            jax.ShapeDtypeStruct((W, FS), BF16),
            jax.ShapeDtypeStruct((FS, W), BF16),
        ),
        in_specs=[vmem] * 3 + [hbm] * 3,
        out_specs=(vmem,) * 5,
        scratch_shapes=[
            pltpu.VMEM((D, FS), BF16),
            pltpu.VMEM((D, FS), BF16),
            pltpu.VMEM((FS, D), BF16),
            pltpu.VMEM((2, 2, 4, GROUP, W), BF16),
            pltpu.VMEM((2, 2, 4, GROUP, W), BF16),
            pltpu.VMEM((3, FS, 4 * GROUP), BF16),
            pltpu.VMEM((2, 4, ROWS, W), BF16),
            pltpu.VMEM((2, 4, GROUP, W), BF16),
            pltpu.VMEM((3, 2, 4, 2 * ROWS, W), BF16),
            pltpu.VMEM((2, 4, ROWS, W), BF16),
            pltpu.VMEM((ROWS, W), F32),
            pltpu.VMEM((2, ROWS // 2, 4 * W), BF16),
            pltpu.VMEM((3, GROUP, FS), BF16),
            pltpu.VMEM((3, GROUP, FS), F32),
            pltpu.VMEM((3, FS, W), BF16),
            pltpu.SemaphoreType.DMA((3,)),
            pltpu.SemaphoreType.DMA((SEMS,)),
            pltpu.SemaphoreType.DMA((SEMS,)),
        ],
        compiler_params=pltpu.CompilerParams(
            collective_id=0, has_side_effects=True, vmem_limit_bytes=62 * 1024 * 1024
        ),
        name="ffn",
    )(modality.reshape(1, -1), tokens, out_grad, gate_weight, up_weight, down_weight)
    results = (out, in_grad, gate_grad, up_grad, down_grad)
    return pl.pallas_call(
        store,
        out_shape=tuple(jax.ShapeDtypeStruct(r.shape, r.dtype) for r in results),
        in_specs=[hbm] * 5,
        out_specs=(hbm,) * 5,
        scratch_shapes=[pltpu.VMEM(r.shape, r.dtype) for r in results] + [pltpu.SemaphoreType.DMA((10,))],
        name="store",
    )(*results)


def solution(mesh):
    return jax.shard_map(
        on_device,
        mesh=mesh,
        in_specs=(
            P(("dp", "seq"), None),
            P(("dp", "seq")),
            P(None, "dp"),
            P(None, "dp"),
            P("dp", None),
            P(("dp", "seq"), None),
        ),
        out_specs=(
            P(("dp", "seq"), None),
            P(("dp", "seq"), None),
            P("seq", "dp"),
            P("seq", "dp"),
            P("dp", "seq"),
        ),
        check_vma=False,
    )
```

time: 178 us -> 137 us (0.77)
  Pallas kernels: 166 us -> 136 us
  local copies, waits for them, and re-layouts: 8.24 us -> 0 us
  other arithmetic: 2.14 us -> 0 us
    pallas_call x1 -> x2, Pallas kernels: 166 us -> 136 us  [the longest x1 133 us: on_device(): pl.pallas_call(body, out_shape=(jax.ShapeDtypeStruct((count, D), BF16), j...]
    squeeze x3 -> x0, local copies, waits for them, and re-layouts: 4.44 us -> none  [on_device(): return (rows[0], rows[1], grads[1].T, grads[2].T, grads[0])]
    unnamed x2 -> x0, local copies, waits for them, and re-layouts: 2.53 us -> none
where the time goes in v2:
time: 137 us
  Pallas kernels  136 us (99%)
    pallas_call x1, Pallas kernels, on_device(): pl.pallas_call(body, out_shape=(jax.ShapeDtypeStruct((count, D), BF16), j...  133 us
    pallas_call x1, Pallas kernels, on_device(): pl.pallas_call(store, out_shape=tuple((jax.ShapeDtypeStruct(r.shape, r.dt...  3.09 us

profile of v2, /device:TPU:1, one launch (start us, length us, event | category | flops | bytes accessed | tf_op | source)
XLA Modules:
  0.0 136.6 jit_solution(5271735832382026944)
XLA Ops:
  0.6 132.8 %ffn.1 = (bf16[24,4096]{1,0:T(8,128)(2,1)}, bf16[24,4096]{1,0:T(8,128)(2,1)}, bf16[512,896]{1,0:T(8,128)(2,1)}, bf16[512,896]{1,0:T(8,128)(2,1)}, bf16[896,512]{1,0:T(8,128)(2,1)}) custom-call(s32[1,32]{1,0:T(1,128)} %bitcast.1, bf16[32,4096]{1,0:T(8,128)(2,1)} %tok_ref.1, bf16[24,4096]{1,0:T(8,128)(2,1)} %cot_ref.1, bf16[4096,896]{1,0:T(8,128)(2,1)} %wg_hbm.1, ...), custom_call_target="tpu_custom_call" | custom-call | tf_op jit(solution)/shard_map/ffn/pallas_call | solution.py:485
  133.4 3.1 %store.1 = (bf16[24,4096]{1,0:T(8,128)(2,1)}, bf16[24,4096]{1,0:T(8,128)(2,1)}, bf16[512,896]{1,0:T(8,128)(2,1)}, bf16[512,896]{1,0:T(8,128)(2,1)}, bf16[896,512]{1,0:T(8,128)(2,1)}) custom-call(bf16[24,4096]{1,0:T(8,128)(2,1)} %get-tuple-element.10.refs_0_, bf16[24,4096]{1,0:T(8,128)(2,1)} %get-tuple-element.11.refs_1_, ...), custom_call_target="tpu_custom_call" | custom-call | tf_op jit(solution)/shard_map/store/pallas_call | solution.py:522

commit v3 on v2

--- a/solution.py
+++ b/solution.py
@@ -234,6 +234,14 @@
         mid[dst] = dot(flat[1, 0, 0], weight[pl.ds(0, W), :])
         lax.fori_loop(1, 8, step, 0)
 
+    def project_gate():
+        loads[0].wait()
+        project(wg, 0)
+
+    def project_up():
+        loads[1].wait()
+        project(wu, 1)
+
     def project_back():
         def step(k, _):
             mid[2] = mid[2] + dot_cols(flat[0, k // 4, k % 4], wd[:, pl.ds(pl.multiple_of(k * W, W), W)])
@@ -362,108 +370,119 @@
         half = pl.ds(pl.multiple_of(c * 4 * W, W), 4 * W)
         to_own[a] = send(final_out.at[a], ref.at[:, half], sibling)
 
+    def settle():
+        for a in (1, 0):
+            to_core[a].wait_send()
+            for copy in to_z[a].values():
+                copy.wait_send()
+        for i in range(len(order)):
+            for copy in (*ring[i], *ring2[i]):
+                copy.wait_send()
+        for gather in (tok_cols, cot_cols):
+            gather.sources_free()
+
     own_rows(1)
     tok_rows.first_y()
     tok_rows.first_z()
-    spread_cols(1)
     own_rows(0)
+    cot_rows.first_y()
     spread_cols(0)
-    cot_rows.first_y()
     tok_rows.stage2()
     start_cols(0, cot_cols)
     tok_rows.stage3()
+    cot_rows.first_z()
     cot_cols.first_z()
+    spread_cols(1)
     tok_rows.stage4()
-    cot_rows.first_z()
+    start_cols(1, tok_cols)
     tok_rows.finish()
+    project_gate()
+    cot_rows.stage2()
+    project_up()
+    tiles(forward)
+    cot_rows.stage3()
+    ring_start(0)
+    cot_cols.stage2()
+    ring_start(1)
     own_cols(1)
-    loads[0].wait()
-    project(wg, 0)
-    cot_cols.stage2()
-    loads[1].wait()
-    project(wu, 1)
-    tiles(forward)
-    ring_start(0)
-    ring_start(1)
-    cot_rows.stage2()
-    cot_cols.stage3()
     rows_free(1, tok_rows)
+    cot_rows.stage4()
     loads[2].wait()
     out_half(other)
+    cot_rows.finish()
+    ring_pass(0)
+    cot_cols.stage3()
+    ring_start(2)
+    project_back()
+    tok_cols.first_z()
+    cot_cols.stage4()
+    out_half(c)
     core_start(1)
-    ring_pass(0)
-    ring_start(2)
-    cot_rows.stage3()
-    cot_cols.stage4()
-    start_cols(1, tok_cols)
-    tok_cols.first_z()
+    own_cols(0)
     ring_pass(1)
+    cot_cols.finish()
+    weight_grad(0)
+    tok_cols.stage2()
     ring_start(3)
-    out_half(c)
-    cot_rows.stage4()
-    cot_rows.finish()
-    own_cols(0)
-    cot_cols.finish()
     ring_pass(2)
-    tok_cols.stage2()
-    weight_grad(0)
-    project_back()
     tiles(backward)
     ring_start(4)
-    ring_start(5)
-    ring_pass(3)
     weight_grad(1)
     tok_cols.stage3()
     rows_free(0, cot_rows)
+    ring_pass(3)
+    core_done(1)
+    weight_grad(2)
+    tok_cols.stage4()
+    weight_done(0)
+    ring_start(5)
     in_half(other)
+    weight_done(1)
+    ring_pass(4)
+    weight_grad(3)
     core_start(0)
-    weight_grad(2)
-    ring_pass(4)
+    ring_pass(5)
     ring_start(6)
-    tok_cols.stage4()
-    core_done(1)
-    weight_grad(3)
-    ring_pass(5)
-    ring_start(7)
     tok_cols.finish()
     weight_grad(4)
     in_half(c)
-    ring_pass(6)
-    ring_start(8)
     weight_grad(5)
     core_done(0)
+    ring_pass(6)
+    weight_done(2)
+    weight_done(3)
+    ring_start(7)
+    weight_done(4)
+    z_done(1)
+    ring_start(8)
     ring_pass(7)
+    weight_grad(6)
     ring_start(9)
-    for i in range(6, 12):
-        weight_grad(i)
-        if i + 2 < 12:
-            ring_pass(i + 2)
-        if i + 4 < 12:
-            ring_start(i + 4)
-        weight_done(i - 6)
-        if i == 6:
-            z_done(1)
-        if i == 8:
-            y_done(1)
-        if i == 9:
-            z_done(0)
-        if i == 11:
-            y_done(0)
-    for i in (6, 7):
-        weight_done(i)
-    for i in range(8, 12):
-        weight_done(i)
+    ring_start(10)
+    weight_grad(7)
+    ring_pass(8)
+    ring_pass(9)
+    ring_start(11)
+    weight_done(5)
+    y_done(1)
+    z_done(0)
+    weight_grad(8)
+    weight_grad(9)
+    weight_done(6)
+    weight_done(7)
+    ring_pass(10)
+    weight_grad(10)
+    ring_pass(11)
+    settle()
+    weight_grad(11)
+    weight_done(8)
+    weight_done(9)
+    y_done(0)
+    weight_done(10)
+    weight_done(11)
     for a in (1, 0):
+        to_y[a].wait_send()
         to_own[a].wait()
-        to_y[a].wait_send()
-        to_core[a].wait_send()
-        for copy in to_z[a].values():
-            copy.wait_send()
-    for i in range(12):
-        for copy in (*ring[i], *ring2[i]):
-            copy.wait_send()
-    for gather in (tok_cols, cot_cols):
-        gather.sources_free()
 
 
 def store(*refs):

time: 137 us -> 138 us (level)
    pallas_call x1, Pallas kernels: 133 us -> 134 us  [on_device(): pl.pallas_call(body, out_shape=(jax.ShapeDtypeStruct((count, D), BF16), j...]
where the time goes in v3:
time: 138 us
  Pallas kernels  137 us (99%)
    pallas_call x1, Pallas kernels, on_device(): pl.pallas_call(body, out_shape=(jax.ShapeDtypeStruct((count, D), BF16), j...  134 us
    pallas_call x1, Pallas kernels, on_device(): pl.pallas_call(store, out_shape=tuple((jax.ShapeDtypeStruct(r.shape, r.dt...  3.09 us

profile of v3, /device:TPU:1, one launch (start us, length us, event | category | flops | bytes accessed | tf_op | source)
XLA Modules:
  0.0 138.1 jit_solution(17048866558006666030)
XLA Ops:
  0.6 134.2 %ffn.1 = (bf16[24,4096]{1,0:T(8,128)(2,1)}, bf16[24,4096]{1,0:T(8,128)(2,1)}, bf16[512,896]{1,0:T(8,128)(2,1)}, bf16[512,896]{1,0:T(8,128)(2,1)}, bf16[896,512]{1,0:T(8,128)(2,1)}) custom-call(s32[1,32]{1,0:T(1,128)} %bitcast.1, bf16[32,4096]{1,0:T(8,128)(2,1)} %tok_ref.1, bf16[24,4096]{1,0:T(8,128)(2,1)} %cot_ref.1, bf16[4096,896]{1,0:T(8,128)(2,1)} %wg_hbm.1, ...), custom_call_target="tpu_custom_call" | custom-call | tf_op jit(solution)/shard_map/ffn/pallas_call | solution.py:504
  134.9 3.1 %store.1 = (bf16[24,4096]{1,0:T(8,128)(2,1)}, bf16[24,4096]{1,0:T(8,128)(2,1)}, bf16[512,896]{1,0:T(8,128)(2,1)}, bf16[512,896]{1,0:T(8,128)(2,1)}, bf16[896,512]{1,0:T(8,128)(2,1)}) custom-call(bf16[24,4096]{1,0:T(8,128)(2,1)} %get-tuple-element.10.refs_0_, bf16[24,4096]{1,0:T(8,128)(2,1)} %get-tuple-element.11.refs_1_, ...), custom_call_target="tpu_custom_call" | custom-call | tf_op jit(solution)/shard_map/store/pallas_call | solution.py:541

commit v4 on v3

--- a/solution.py
+++ b/solution.py
@@ -198,7 +198,7 @@
             return cols.at[a, c, pl.ds(1, 3), rows(q), lanes]
         return chunk
 
-    tok_rows, cot_rows = GatherZ(row_chunk(1)), GatherZ(row_chunk(0))
+    tok_rows, cot_rows = GatherZ(row_chunk(1)), Gather(row_chunk(0))
     tok_cols, cot_cols = GatherZ(col_chunk(1)), GatherZ(col_chunk(0))
     spread = {1: [], 0: []}
 
@@ -382,102 +382,102 @@
             gather.sources_free()
 
     own_rows(1)
+    tok_rows.first_z()
     tok_rows.first_y()
-    tok_rows.first_z()
     own_rows(0)
-    cot_rows.first_y()
+    spread_cols(1)
     spread_cols(0)
     tok_rows.stage2()
+    tok_rows.stage3()
+    cot_rows.first_y()
     start_cols(0, cot_cols)
-    tok_rows.stage3()
+    start_cols(1, tok_cols)
     cot_rows.first_z()
+    tok_rows.stage4()
     cot_cols.first_z()
-    spread_cols(1)
-    tok_rows.stage4()
-    start_cols(1, tok_cols)
     tok_rows.finish()
     project_gate()
     cot_rows.stage2()
+    cot_cols.stage2()
     project_up()
     tiles(forward)
+    tok_cols.first_z()
+    ring_start(0)
+    loads[2].wait()
+    own_cols(1)
+    cot_cols.stage3()
     cot_rows.stage3()
-    ring_start(0)
-    cot_cols.stage2()
     ring_start(1)
-    own_cols(1)
     rows_free(1, tok_rows)
+    out_half(c)
+    out_half(other)
     cot_rows.stage4()
-    loads[2].wait()
-    out_half(other)
+    ring_pass(0)
+    tok_cols.stage2()
+    cot_cols.stage4()
+    ring_start(2)
+    ring_start(3)
+    core_start(1)
     cot_rows.finish()
-    ring_pass(0)
-    cot_cols.stage3()
-    ring_start(2)
     project_back()
-    tok_cols.first_z()
-    cot_cols.stage4()
-    out_half(c)
-    core_start(1)
+    cot_cols.finish()
     own_cols(0)
+    weight_grad(0)
     ring_pass(1)
-    cot_cols.finish()
-    weight_grad(0)
-    tok_cols.stage2()
-    ring_start(3)
+    tiles(backward)
     ring_pass(2)
-    tiles(backward)
     ring_start(4)
     weight_grad(1)
+    weight_done(0)
     tok_cols.stage3()
+    core_done(1)
+    ring_start(5)
+    weight_grad(2)
     rows_free(0, cot_rows)
     ring_pass(3)
-    core_done(1)
-    weight_grad(2)
     tok_cols.stage4()
-    weight_done(0)
-    ring_start(5)
+    ring_pass(4)
     in_half(other)
-    weight_done(1)
-    ring_pass(4)
     weight_grad(3)
+    ring_pass(5)
     core_start(0)
-    ring_pass(5)
-    ring_start(6)
     tok_cols.finish()
     weight_grad(4)
+    ring_start(6)
     in_half(c)
+    ring_start(7)
+    ring_start(8)
+    weight_done(1)
     weight_grad(5)
+    ring_pass(6)
     core_done(0)
-    ring_pass(6)
+    ring_pass(7)
+    z_done(1)
     weight_done(2)
+    ring_start(9)
     weight_done(3)
-    ring_start(7)
+    weight_grad(6)
+    ring_pass(8)
     weight_done(4)
-    z_done(1)
-    ring_start(8)
-    ring_pass(7)
-    weight_grad(6)
-    ring_start(9)
+    weight_done(5)
     ring_start(10)
     weight_grad(7)
-    ring_pass(8)
+    weight_grad(8)
+    ring_start(11)
+    z_done(0)
     ring_pass(9)
-    ring_start(11)
-    weight_done(5)
-    y_done(1)
-    z_done(0)
-    weight_grad(8)
+    ring_pass(10)
     weight_grad(9)
-    weight_done(6)
-    weight_done(7)
-    ring_pass(10)
     weight_grad(10)
     ring_pass(11)
+    y_done(1)
+    weight_done(6)
     settle()
     weight_grad(11)
+    weight_done(7)
     weight_done(8)
+    y_done(0)
     weight_done(9)
-    y_done(0)
     weight_done(10)
     weight_done(11)
     for a in (1, 0):

time: 138 us -> 135 us (0.978)
  Pallas kernels: 137 us -> 134 us
    pallas_call x1, Pallas kernels: 134 us -> 131 us  [on_device(): pl.pallas_call(body, out_shape=(jax.ShapeDtypeStruct((count, D), BF16), j...]
where the time goes in v4:
time: 135 us
  Pallas kernels  134 us (99%)
    pallas_call x1, Pallas kernels, on_device(): pl.pallas_call(body, out_shape=(jax.ShapeDtypeStruct((count, D), BF16), j...  131 us
    pallas_call x1, Pallas kernels, on_device(): pl.pallas_call(store, out_shape=tuple((jax.ShapeDtypeStruct(r.shape, r.dt...  3.09 us

profile of v4, /device:TPU:1, one launch (start us, length us, event | category | flops | bytes accessed | tf_op | source)
XLA Modules:
  0.0 135.1 jit_solution(7011846019510348731)
XLA Ops:
  0.6 131.2 %ffn.1 = (bf16[24,4096]{1,0:T(8,128)(2,1)}, bf16[24,4096]{1,0:T(8,128)(2,1)}, bf16[512,896]{1,0:T(8,128)(2,1)}, bf16[512,896]{1,0:T(8,128)(2,1)}, bf16[896,512]{1,0:T(8,128)(2,1)}) custom-call(s32[1,32]{1,0:T(1,128)} %bitcast.1, bf16[32,4096]{1,0:T(8,128)(2,1)} %tok_ref.1, bf16[24,4096]{1,0:T(8,128)(2,1)} %cot_ref.1, bf16[4096,896]{1,0:T(8,128)(2,1)} %wg_hbm.1, ...), custom_call_target="tpu_custom_call" | custom-call | tf_op jit(solution)/shard_map/ffn/pallas_call | solution.py:504
  131.8 3.1 %store.1 = (bf16[24,4096]{1,0:T(8,128)(2,1)}, bf16[24,4096]{1,0:T(8,128)(2,1)}, bf16[512,896]{1,0:T(8,128)(2,1)}, bf16[512,896]{1,0:T(8,128)(2,1)}, bf16[896,512]{1,0:T(8,128)(2,1)}) custom-call(bf16[24,4096]{1,0:T(8,128)(2,1)} %get-tuple-element.10.refs_0_, bf16[24,4096]{1,0:T(8,128)(2,1)} %get-tuple-element.11.refs_1_, ...), custom_call_target="tpu_custom_call" | custom-call | tf_op jit(solution)/shard_map/store/pallas_call | solution.py:541
